TPU v7x, 32 devices: a whole 2x2x4 slice. The times are simulated.
32 devices in a mesh: segment: 2 (over core), dp: 4 (over y, x), mp: 4 (over z).
Axes of the slice: x: 2, y: 2, z: 4, core: 2. Of those that a mesh axis runs over, the one named last changes fastest.
Arguments:
- token_ids: int32 [2, 256], replicated, may hold values from 0 to 32767
- table: bfloat16 [32768, 8192], P('dp', 'mp'), may hold values from -6 to 6
- w_up: bfloat16 [2, 8192, 32768], P('segment', 'mp', 'dp'), may hold values from -0.0625 to 0.0625
- w_down: bfloat16 [2, 32768, 8192], P('segment', 'dp', 'mp'), may hold values from -0.03125 to 0.03125
- cotangent: bfloat16 [2, 256, 8192], P(None, 'dp', 'mp'), may hold values from -6 to 6
Outputs:
- acts: bfloat16 [2, 2, 256, 8192], P('segment', None, 'dp', 'mp')
- grads: bfloat16 [2, 2, 256, 8192], P('segment', None, 'dp', 'mp')
All inputs are finite; a program needn't handle non-finite values.
Results may differ from a plain program's by a relative error of at most 0.018.
Values may be sent and summed in bfloat16 or wider, within the bound.
A program may use at most 192 MiB of HBM per device.

v0:
```python
from functools import partial
import jax
import jax.numpy as jnp
from jax import lax
from jax.sharding import PartitionSpec as P

root_coef = 0.7978845608028654


def from_behind(value, axis, steps):
    count = lax.axis_size(axis)
    leading, last = (max(0, -steps), min(count, count - steps))
    return lax.ppermute(value, axis, [(source, source + steps) for source in range(leading, last)])


def gelu_value(value):
    return 0.5 * value * (1.0 + jnp.tanh(root_coef * (value + 0.044715 * value * value * value)))


def gelu_slope(value):
    inner = jnp.tanh(root_coef * (value + 0.044715 * value * value * value))
    return 0.5 * (1.0 + inner) + 0.5 * value * (1.0 - inner * inner) * root_coef * (
        1.0 + 0.134145 * value * value
    )


def forward_activate(summed):
    return (gelu_value(summed).astype(jnp.bfloat16), summed)


def backward_activate(saved, summed):
    return ((gelu_slope(saved) * summed).astype(jnp.bfloat16), saved)


def lookup(token_row, table):
    table_rows = table.shape[0]
    offset = lax.axis_index("dp") * table_rows
    picked = token_row - offset
    inside = (picked >= 0) & (picked < table_rows)
    fetched = jnp.take(table, jnp.clip(picked, 0, table_rows - 1), axis=0)
    return lax.psum_scatter(
        jnp.where(inside[:, None], fetched.astype(jnp.float32), 0.0).astype(jnp.bfloat16),
        "dp",
        scatter_dimension=0,
        tiled=True,
    )


def layer_pass(inputs, first_weight, first_dim, second_weight, second_dim, activate):
    partial_sum = lax.dot_general(
        lax.all_gather(inputs, "dp", axis=0, tiled=True),
        first_weight,
        (((1,), (first_dim,)), ((), ())),
        preferred_element_type=jnp.float32,
    )
    summed = lax.psum(partial_sum.astype(jnp.bfloat16), "mp").astype(jnp.float32)
    active, kept = activate(summed)
    mixed = lax.psum_scatter(
        lax.dot_general(
            active,
            second_weight,
            (((1,), (second_dim,)), ((), ())),
            preferred_element_type=jnp.float32,
        ).astype(jnp.bfloat16),
        "dp",
        scatter_dimension=0,
        tiled=True,
    ).astype(jnp.float32)
    return ((inputs.astype(jnp.float32) + mixed).astype(jnp.bfloat16), kept)


def on_device(token_ids, table, w_up, w_down, cotangent):
    micro_count = cotangent.shape[0]
    up_local = w_up[0]
    down_local = w_down[0]
    is_first = lax.axis_index("segment") == 0
    received = jnp.zeros(cotangent.shape[1:], jnp.bfloat16)
    kept_list = []
    forward_outs = []
    for tick in range(micro_count + 1):
        if tick < micro_count:
            entering = lookup(token_ids[tick], table)
        else:
            entering = jnp.zeros_like(received)
        inputs = jnp.where(is_first, entering, received)
        leaving, kept = layer_pass(inputs, up_local, 0, down_local, 0, forward_activate)
        kept_list.append(kept)
        forward_outs.append(leaving)
        if tick < micro_count:
            received = from_behind(leaving, "segment", 1)
    returned = jnp.zeros_like(received)
    backward_outs = []
    for tick in range(micro_count + 1):
        if tick < micro_count:
            given = cotangent[micro_count - 1 - tick]
        else:
            given = jnp.zeros_like(received)
        upstream = jnp.where(is_first, returned, given)
        activate = partial(backward_activate, kept_list[micro_count - tick])
        gradient, unused = layer_pass(upstream, down_local, 1, up_local, 1, activate)
        backward_outs.append(gradient)
        if tick < micro_count:
            returned = from_behind(gradient, "segment", -1)
    acts = jnp.stack(
        [
            jnp.where(is_first, forward_outs[micro_pos], forward_outs[micro_pos + 1])
            for micro_pos in range(micro_count)
        ]
    )
    grads = jnp.stack(
        [
            jnp.where(
                is_first,
                backward_outs[micro_count - micro_pos],
                backward_outs[micro_count - 1 - micro_pos],
            )
            for micro_pos in range(micro_count)
        ]
    )
    return (acts[None], grads[None])


def solution(mesh):
    return jax.shard_map(
        on_device,
        mesh=mesh,
        in_specs=(
            P(),
            P("dp", "mp"),
            P("segment", "mp", "dp"),
            P("segment", "dp", "mp"),
            P(None, "dp", "mp"),
        ),
        out_specs=(P("segment", None, "dp", "mp"), P("segment", None, "dp", "mp")),
        check_vma=False,
    )
```

profile of v0, /device:TPU:0, one launch (start us, length us, event | category | flops | bytes accessed | tf_op | source)
XLA Modules:
  0.0 1510.9 jit_solution(5395322229420565547)
XLA Ops:
  7.2 0.8 and_reduce_fusion.1
  8.0 0.8 broadcast_clamp_fusion
  8.8 10.1 gather_fusion
  19.0 1.3 select_convert_fusion.1
  20.3 0.0 all-gather.8.cloned.1.call-start
  20.3 31.3 %reduce-scatter.9.cloned.1.call-done = bf16[64,2048]{1,0:T(8,128)(2,1)} async-done(((bf16[256,2048]{1,0:T(8,128)(2,1)}), bf16[64,2048]{1,0:T(8,128)(2,1)}) %reduce-scatter.9.cloned.1.call-update) | async-done | bytes 262160 | tf_op jit(solution)/shard_map/reduce_scatter | solution.py:41
  51.7 1.7 broadcast_select_fusion.3
  53.4 27.2 %all-gather.8.cloned.1.call-done = bf16[256,2048]{1,0:T(8,128)(2,1)} async-done(((bf16[64,2048]{1,0:T(8,128)(2,1)}), bf16[256,2048]{1,0:T(8,128)(2,1)}) %all-gather.8.cloned.1.call-update) | async-done | bytes 1048592 | tf_op jit(solution)/shard_map/all_gather | solution.py:51
  80.6 16.7 %fusion.24 = bf16[256,8192]{1,0:T(8,128)(2,1)} fusion(bf16[256,2048]{1,0:T(8,128)(2,1)} %all-gather.8.cloned.1.call-done, bf16[1,2048,8192]{2,1,0:T(8,128)(2,1)} %param.9), kind=kOutput, calls=%fused_computation.47 | convolution fusion | flops 8592031744 | bytes 38797312 | tf_op jit(solution)/shard_map/dot_general | solution.py:50
  97.4 155.1 %all-reduce.7.cloned.1.call-done = bf16[256,8192]{1,0:T(8,128)(2,1)} async-done(((bf16[256,8192]{1,0:T(8,128)(2,1)}), bf16[256,8192]{1,0:T(8,128)(2,1)}) %all-reduce.7.cloned.1.call-update) | async-done | bytes 4194320 | tf_op jit(solution)/shard_map/psum | solution.py:56
  252.5 18.7 %fusion.123 = bf16[256,2048]{1,0:T(8,128)(2,1)} fusion(bf16[1,8192,2048]{2,1,0:T(8,128)(2,1)} %param.10, bf16[256,8192]{1,0:T(8,128)(2,1)} %all-reduce.7.cloned.1.call-done), kind=kOutput, calls=%fused_computation.116 | convolution fusion | flops 8611430400 | bytes 38797312 | tf_op jit(solution)/shard_map/dot_general | solution.py:59
  271.3 0.2 reduce-scatter.13.cloned.1.call-start
  271.5 10.3 gather_fusion.1
  281.8 1.3 select_convert_fusion
  283.2 15.1 reduce-scatter.11.cloned.1.call-done
  298.3 1.0 add_convert_fusion.4
  299.4 1.6 collective-permute-start
  301.0 28.1 %reduce-scatter.13.cloned.1.call-done = bf16[64,2048]{1,0:T(8,128)(2,1)} async-done(((bf16[256,2048]{1,0:T(8,128)(2,1)}), bf16[64,2048]{1,0:T(8,128)(2,1)}) %reduce-scatter.13.cloned.1.call-update) | async-done | bytes 262160 | tf_op jit(solution)/shard_map/reduce_scatter | solution.py:41
  329.0 1.7 broadcast_select_fusion.2
  330.8 27.0 %all-gather.10.cloned.1.call-done = bf16[256,2048]{1,0:T(8,128)(2,1)} async-done(((bf16[64,2048]{1,0:T(8,128)(2,1)}), bf16[256,2048]{1,0:T(8,128)(2,1)}) %all-gather.10.cloned.1.call-update) | async-done | bytes 1048592 | tf_op jit(solution)/shard_map/all_gather | solution.py:51
  357.8 16.6 %fusion.27 = bf16[256,8192]{1,0:T(8,128)(2,1)} fusion(bf16[256,2048]{1,0:T(8,128)(2,1)} %all-gather.10.cloned.1.call-done, bf16[1,2048,8192]{2,1,0:T(8,128)(2,1)} %param.9), kind=kOutput, calls=%fused_computation.48 | convolution fusion | flops 8592031744 | bytes 38797312 | tf_op jit(solution)/shard_map/dot_general | solution.py:50
  374.6 155.1 %all-reduce.9.cloned.1.call-done = bf16[256,8192]{1,0:T(8,128)(2,1)} async-done(((bf16[256,8192]{1,0:T(8,128)(2,1)}), bf16[256,8192]{1,0:T(8,128)(2,1)}) %all-reduce.9.cloned.1.call-update) | async-done | bytes 4194320 | tf_op jit(solution)/shard_map/psum | solution.py:56
  529.6 18.7 %fusion.128 = bf16[256,2048]{1,0:T(8,128)(2,1)} fusion(bf16[1,8192,2048]{2,1,0:T(8,128)(2,1)} %param.10, bf16[256,8192]{1,0:T(8,128)(2,1)} %all-reduce.9.cloned.1.call-done), kind=kOutput, calls=%fused_computation.117 | convolution fusion | flops 8611430400 | bytes 38797312 | tf_op jit(solution)/shard_map/dot_general | solution.py:59
  548.4 0.7 slice_select_fusion
  549.3 26.2 %reduce-scatter.15.cloned.1.call-done = bf16[64,2048]{1,0:T(8,128)(2,1)} async-done(((bf16[256,2048]{1,0:T(8,128)(2,1)}), bf16[64,2048]{1,0:T(8,128)(2,1)}) %reduce-scatter.15.cloned.1.call-update) | async-done | bytes 262160 | tf_op jit(solution)/shard_map/reduce_scatter | solution.py:58
  575.5 1.8 select_bitcast_fusion.1
  577.2 0.7 copy-done.4
  577.9 1.8 collective-permute-start.1
  579.7 1.1 collective-permute-done.1
  580.8 0.7 copy-done.6
  581.5 0.7 broadcast_select_fusion.1
  582.3 21.5 %all-gather.18.cloned.1.call-done = bf16[1,256,2048]{2,1,0:T(8,128)(2,1)} async-done(((bf16[1,64,2048]{2,1,0:T(8,128)(2,1)}), bf16[1,256,2048]{2,1,0:T(8,128)(2,1)}) %all-gather.18.cloned.1.call-update) | async-done | bytes 1048592 | tf_op jit(solution)/shard_map/all_gather | solution.py:51
  603.8 17.2 %fusion.33 = bf16[256,8192]{1,0:T(8,128)(2,1)} fusion(bf16[1,8192,2048]{2,1,0:T(8,128)(2,1)} %param.10, bf16[1,256,2048]{2,1,0:T(8,128)(2,1)} %all-gather.18.cloned.1.call-done), kind=kOutput, calls=%fused_computation.50 | convolution fusion | flops 8592031744 | bytes 38797312 | tf_op jit(solution)/shard_map/dot_general | solution.py:50
  621.0 11.0 all-gather.12.cloned.1.call-done
  632.0 16.7 %fusion.30 = bf16[256,8192]{1,0:T(8,128)(2,1)} fusion(bf16[256,2048]{1,0:T(8,128)(2,1)} %all-gather.12.cloned.1.call-done, bf16[1,2048,8192]{2,1,0:T(8,128)(2,1)} %param.9), kind=kOutput, calls=%fused_computation.49 | convolution fusion | flops 8592031744 | bytes 38797312 | tf_op jit(solution)/shard_map/dot_general | solution.py:50
  648.8 291.0 %all-reduce.15.cloned.1.call-done = (bf16[256,8192]{1,0:T(8,128)(2,1)}, bf16[256,8192]{1,0:T(8,128)(2,1)}) async-done(((bf16[256,8192]{1,0:T(8,128)(2,1)}, bf16[256,8192]{1,0:T(8,128)(2,1)}), (bf16[256,8192]{1,0:T(8,128)(2,1)}, bf16[256,8192]{1,0:T(8,128)(2,1)})) %all-reduce.15.cloned.1.call-update) | async-done | bytes 8388624 | tf_op jit(solution)/shard_map/psum | solution.py:56
  939.8 19.9 %fusion.108 = bf16[256,2048]{1,0:T(8,128)(2,1)} fusion(bf16[1,2048,8192]{2,1,0:T(8,128)(2,1)} %param.9, bf16[256,8192]{1,0:T(8,128)(2,1)} %get-tuple-element.5, bf16[256,8192]{1,0:T(8,128)(2,1)} %get-tuple-element.6), kind=kOutput, calls=%fused_computation.113 | convolution fusion | flops 8634499072 | bytes 42991616 | tf_op jit(solution)/shard_map/dot_general | solution.py:59
  959.8 27.0 %reduce-scatter.19.cloned.1.call-done = bf16[64,2048]{1,0:T(8,128)(2,1)} async-done(((bf16[256,2048]{1,0:T(8,128)(2,1)}), bf16[64,2048]{1,0:T(8,128)(2,1)}) %reduce-scatter.19.cloned.1.call-update) | async-done | bytes 262160 | tf_op jit(solution)/shard_map/reduce_scatter | solution.py:58
  986.8 1.0 fusion.139
  987.9 1.3 collective-permute-start.2
  989.2 2.1 collective-permute-done.2
  991.3 0.7 bitcast_select_fusion
  992.1 0.4 all-reduce.11.cloned.1.call-start
  992.5 26.2 %all-gather.14.cloned.1.call-done = bf16[256,2048]{1,0:T(8,128)(2,1)} async-done(((bf16[64,2048]{1,0:T(8,128)(2,1)}), bf16[256,2048]{1,0:T(8,128)(2,1)}) %all-gather.14.cloned.1.call-update) | async-done | bytes 1048592 | tf_op jit(solution)/shard_map/all_gather | solution.py:51
  1018.7 16.9 %fusion.36 = bf16[256,8192]{1,0:T(8,128)(2,1)} fusion(bf16[256,2048]{1,0:T(8,128)(2,1)} %all-gather.14.cloned.1.call-done, bf16[1,8192,2048]{2,1,0:T(8,128)(2,1)} %param.10), kind=kOutput, calls=%fused_computation.51 | convolution fusion | flops 8592031744 | bytes 38797312 | tf_op jit(solution)/shard_map/dot_general | solution.py:50
  1035.7 155.1 %all-reduce.11.cloned.1.call-done = bf16[256,8192]{1,0:T(8,128)(2,1)} async-done(((bf16[256,8192]{1,0:T(8,128)(2,1)}), bf16[256,8192]{1,0:T(8,128)(2,1)}) %all-reduce.11.cloned.1.call-update) | async-done | bytes 4194320 | tf_op jit(solution)/shard_map/psum | solution.py:56
  1190.8 19.9 %fusion.113 = bf16[256,2048]{1,0:T(8,128)(2,1)} fusion(bf16[1,2048,8192]{2,1,0:T(8,128)(2,1)} %param.9, bf16[256,8192]{1,0:T(8,128)(2,1)} %all-reduce.9.cloned.1.call-done, bf16[256,8192]{1,0:T(8,128)(2,1)} %all-reduce.11.cloned.1.call-done), kind=kOutput, calls=%fused_computation.114 | convolution fusion | flops 8634499072 | bytes 42991616 | tf_op jit(solution)/shard_map/dot_general | solution.py:59
  1210.8 27.0 %reduce-scatter.21.cloned.1.call-done = bf16[64,2048]{1,0:T(8,128)(2,1)} async-done(((bf16[256,2048]{1,0:T(8,128)(2,1)}), bf16[64,2048]{1,0:T(8,128)(2,1)}) %reduce-scatter.21.cloned.1.call-update) | async-done | bytes 262160 | tf_op jit(solution)/shard_map/reduce_scatter | solution.py:58
  1237.8 1.1 select_bitcast_fusion
  1238.9 1.3 collective-permute-start.3
  1240.2 2.1 collective-permute-done.3
  1242.3 0.7 broadcast_select_fusion
  1243.1 26.6 %all-gather.16.cloned.1.call-done = bf16[256,2048]{1,0:T(8,128)(2,1)} async-done(((bf16[64,2048]{1,0:T(8,128)(2,1)}), bf16[256,2048]{1,0:T(8,128)(2,1)}) %all-gather.16.cloned.1.call-update) | async-done | bytes 1048592 | tf_op jit(solution)/shard_map/all_gather | solution.py:51
  1269.7 16.9 %fusion.39 = bf16[256,8192]{1,0:T(8,128)(2,1)} fusion(bf16[256,2048]{1,0:T(8,128)(2,1)} %all-gather.16.cloned.1.call-done, bf16[1,8192,2048]{2,1,0:T(8,128)(2,1)} %param.10), kind=kOutput, calls=%fused_computation.52 | convolution fusion | flops 8592031744 | bytes 38797312 | tf_op jit(solution)/shard_map/dot_general | solution.py:50
  1286.6 0.2 reduce-scatter.17.cloned.1.call-start
  1286.9 19.5 %fusion.133 = bf16[256,2048]{1,0:T(8,128)(2,1)} fusion(bf16[1,8192,2048]{2,1,0:T(8,128)(2,1)} %param.10, bf16[256,8192]{1,0:T(8,128)(2,1)} %get-tuple-element.5), kind=kOutput, calls=%fused_computation.118 | convolution fusion | flops 8611430400 | bytes 38797312 | tf_op jit(solution)/shard_map/dot_general | solution.py:59
  1306.5 135.3 %all-reduce.13.cloned.1.call-done = bf16[256,8192]{1,0:T(8,128)(2,1)} async-done(((bf16[256,8192]{1,0:T(8,128)(2,1)}), bf16[256,8192]{1,0:T(8,128)(2,1)}) %all-reduce.13.cloned.1.call-update) | async-done | bytes 4194320 | tf_op jit(solution)/shard_map/psum | solution.py:56
  1441.8 20.2 %fusion.118 = bf16[256,2048]{1,0:T(8,128)(2,1)} fusion(bf16[1,2048,8192]{2,1,0:T(8,128)(2,1)} %param.9, bf16[256,8192]{1,0:T(8,128)(2,1)} %all-reduce.7.cloned.1.call-done, bf16[256,8192]{1,0:T(8,128)(2,1)} %all-reduce.13.cloned.1.call-done), kind=kOutput, calls=%fused_computation.115 | convolution fusion | flops 8634499072 | bytes 42991616 | tf_op jit(solution)/shard_map/dot_general | solution.py:59
  1462.0 9.5 reduce-scatter.17.cloned.1.call-done
  1471.5 1.1 fusion.141
  1472.5 0.8 maximum_bitcast_fusion
  1473.4 28.9 %reduce-scatter.23.cloned.1.call-done = bf16[64,2048]{1,0:T(8,128)(2,1)} async-done(((bf16[256,2048]{1,0:T(8,128)(2,1)}), bf16[64,2048]{1,0:T(8,128)(2,1)}) %reduce-scatter.23.cloned.1.call-update) | async-done | bytes 262160 | tf_op jit(solution)/shard_map/reduce_scatter | solution.py:58
  1502.3 1.1 fusion.143
  1503.4 0.8 maximum_bitcast_fusion.1
  (57 shorter events, 1.0 us)
Async XLA Ops:
  7.2 44.5 %reduce-scatter.9.cloned.1.call-start = ((), (), s32[]{:S(2)}) async-start(), calls=%async_computation.8 | async-start | bytes 1310720 | tf_op jit(solution)/shard_map/reduce_scatter | solution.py:41
  20.3 60.3 %all-gather.8.cloned.1.call-start = ((), (), s32[]{:S(2)}) async-start(), calls=%async_computation.9 | async-start | bytes 1310720 | tf_op jit(solution)/shard_map/all_gather | solution.py:51
  53.4 199.1 %all-reduce.7.cloned.1.call-start = ((), (), s32[]{:S(2)}) async-start(), calls=%async_computation.10 | async-start | bytes 8388608 | tf_op jit(solution)/shard_map/psum | solution.py:56
  97.4 201.0 %reduce-scatter.11.cloned.1.call-start = ((), (), s32[]{:S(2)}) async-start(), calls=%async_computation.11 | async-start | bytes 1310720 | tf_op jit(solution)/shard_map/reduce_scatter | solution.py:58
  271.2 27.1 %copy-start.8 = (bf16[64,2048]{1,0:T(8,128)(2,1)S(1)}, bf16[64,2048]{1,0:T(8,128)(2,1)}, u32[]{:S(2)}) copy-start(bf16[64,2048]{1,0:T(8,128)(2,1)} %reduce-scatter.9.cloned.1.call-done) | copy-start | bytes 786436
  271.3 57.8 %reduce-scatter.13.cloned.1.call-start = ((), (), s32[]{:S(2)}) async-start(), calls=%async_computation.12 | async-start | bytes 1310720 | tf_op jit(solution)/shard_map/reduce_scatter | solution.py:41
  283.2 74.7 %all-gather.10.cloned.1.call-start = ((), (), s32[]{:S(2)}) async-start(), calls=%async_computation.13 | async-start | bytes 1310720 | tf_op jit(solution)/shard_map/all_gather | solution.py:51
  299.4 29.7 %collective-permute-start = (bf16[64,2048]{1,0:T(8,128)(2,1)S(1)}, bf16[64,2048]{1,0:T(8,128)(2,1)S(1)}, u32[]{:S(2)}, u32[]{:S(2)}) collective-permute-start(bf16[64,2048]{1,0:T(8,128)(2,1)S(1)} %add_convert_fusion.4), channel_id=1, source_target_pairs={{0,16},{1,17},{2,18},{3,19},{4,20},{5,21},{6,22},{7,23},{8,24},{9,... | collective-permute-start | bytes 786440 | tf_op jit(solution)/shard_map/ppermute | solution.py:13
  330.7 198.9 %all-reduce.9.cloned.1.call-start = ((), (), s32[]{:S(2)}) async-start(), calls=%async_computation.14 | async-start | bytes 8388608 | tf_op jit(solution)/shard_map/psum | solution.py:56
  374.5 173.9 %copy-start.2 = (bf16[2,64,2048]{2,1,0:T(8,128)(2,1)S(1)}, bf16[2,64,2048]{2,1,0:T(8,128)(2,1)}, u32[]{:S(2)}) copy-start(bf16[2,64,2048]{2,1,0:T(8,128)(2,1)} %param.11) | copy-start | bytes 1572868
  374.5 201.0 %copy-start = (bf16[64,2048]{1,0:T(8,128)(2,1)S(1)}, bf16[64,2048]{1,0:T(8,128)(2,1)}, u32[]{:S(2)}) copy-start(bf16[64,2048]{1,0:T(8,128)(2,1)} %broadcast_select_fusion.2) | copy-start | bytes 786436
  374.5 200.9 %reduce-scatter.15.cloned.1.call-start = ((), (), s32[]{:S(2)}) async-start(), calls=%async_computation.15 | async-start | bytes 1310720 | tf_op jit(solution)/shard_map/reduce_scatter | solution.py:58
  548.4 55.4 %all-gather.18.cloned.1.call-start = ((), (), s32[]{:S(2)}) async-start(), calls=%async_computation.25 | async-start | bytes 1310720 | tf_op jit(solution)/shard_map/all_gather | solution.py:51
  549.2 82.8 %all-gather.12.cloned.1.call-start = ((), (), s32[]{:S(2)}) async-start(), calls=%async_computation.16 | async-start | bytes 1310720 | tf_op jit(solution)/shard_map/all_gather | solution.py:51
  577.2 0.7 copy-start.4
  577.9 2.9 collective-permute-start.1
  580.8 0.7 copy-start.6
  582.3 357.5 %all-reduce.15.cloned.1.call-start = ((), (), s32[]{:S(2)}) async-start(), calls=%async_computation.26 | async-start | bytes 16777216 | tf_op jit(solution)/shard_map/psum | solution.py:56
  648.8 338.0 %reduce-scatter.19.cloned.1.call-start = ((), (), s32[]{:S(2)}) async-start(), calls=%async_computation.18 | async-start | bytes 1310720 | tf_op jit(solution)/shard_map/reduce_scatter | solution.py:58
  959.7 59.0 %all-gather.14.cloned.1.call-start = ((), (), s32[]{:S(2)}) async-start(), calls=%async_computation.19 | async-start | bytes 1310720 | tf_op jit(solution)/shard_map/all_gather | solution.py:51
  987.9 3.4 collective-permute-start.2
  992.1 198.8 %all-reduce.11.cloned.1.call-start = ((), (), s32[]{:S(2)}) async-start(), calls=%async_computation.20 | async-start | bytes 8388608 | tf_op jit(solution)/shard_map/psum | solution.py:56
  1035.7 202.1 %copy-start.1 = (bf16[64,2048]{1,0:T(8,128)(2,1)S(1)}, bf16[64,2048]{1,0:T(8,128)(2,1)}, u32[]{:S(2)}) copy-start(bf16[64,2048]{1,0:T(8,128)(2,1)} %bitcast_select_fusion) | copy-start | bytes 786436
  1035.7 202.1 %reduce-scatter.21.cloned.1.call-start = ((), (), s32[]{:S(2)}) async-start(), calls=%async_computation.21 | async-start | bytes 1310720 | tf_op jit(solution)/shard_map/reduce_scatter | solution.py:58
  1210.7 59.0 %all-gather.16.cloned.1.call-start = ((), (), s32[]{:S(2)}) async-start(), calls=%async_computation.22 | async-start | bytes 1310720 | tf_op jit(solution)/shard_map/all_gather | solution.py:51
  1238.9 3.4 collective-permute-start.3
  1243.1 198.7 %all-reduce.13.cloned.1.call-start = ((), (), s32[]{:S(2)}) async-start(), calls=%async_computation.23 | async-start | bytes 8388608 | tf_op jit(solution)/shard_map/psum | solution.py:56
  1286.6 184.8 %reduce-scatter.17.cloned.1.call-start = ((), (), s32[]{:S(2)}) async-start(), calls=%async_computation.17 | async-start | bytes 1310720 | tf_op jit(solution)/shard_map/reduce_scatter | solution.py:58
  1306.4 165.1 %copy-start.5 = (bf16[64,2048]{1,0:T(8,128)(2,1)S(1)}, bf16[64,2048]{1,0:T(8,128)(2,1)}, u32[]{:S(2)}) copy-start(bf16[64,2048]{1,0:T(8,128)(2,1)} %copy-done.4) | copy-start | bytes 786436
  1306.4 165.0 %copy-start.7 = (bf16[64,2048]{1,0:T(8,128)(2,1)S(1)}, bf16[64,2048]{1,0:T(8,128)(2,1)}, u32[]{:S(2)}) copy-start(bf16[64,2048]{1,0:T(8,128)(2,1)} %copy-done.6) | copy-start | bytes 786436
  1306.4 166.1 %copy-start.3 = (bf16[1,64,2048]{2,1,0:T(8,128)(2,1)S(1)}, bf16[1,64,2048]{2,1,0:T(8,128)(2,1)}, u32[]{:S(2)}) copy-start(bf16[1,64,2048]{2,1,0:T(8,128)(2,1)} %get-tuple-element.9) | copy-start | bytes 786436
  1306.4 195.9 %reduce-scatter.23.cloned.1.call-start = ((), (), s32[]{:S(2)}) async-start(), calls=%async_computation.24 | async-start | bytes 1310720 | tf_op jit(solution)/shard_map/reduce_scatter | solution.py:58
Sparse Core Ops, SparseCore 0:
  20.4 31.2 reduce-scatter.8
  54.1 26.4 all-gather.7
  97.5 154.9 all-reduce.6
  271.4 26.9 reduce-scatter.10
  301.1 27.9 reduce-scatter.12
  331.3 26.4 all-gather.9
  374.6 154.9 all-reduce.8
  548.5 26.9 reduce-scatter.14
  577.3 26.4 all-gather.17
  605.5 26.4 all-gather.11
  648.9 290.8 all-reduce.14
  959.9 26.9 reduce-scatter.18
  992.2 26.4 all-gather.13
  1035.8 154.9 all-reduce.10
  1210.9 26.9 reduce-scatter.20
  1243.2 26.4 all-gather.15
  1286.8 154.9 all-reduce.12
  1444.5 26.9 reduce-scatter.16
  1474.4 27.9 reduce-scatter.22
where the time goes:
time: 1520 us; the launch traced here: 1510 us
  waiting for transfers between devices  1230 us (81%)
  matrix products  218 us (14%)
  local copies, waits for them, and re-layouts  21.9 us (1%)
  other arithmetic  19.2 us (1%)
    psum x5, waiting for transfers between devices, layer_pass(): lax.psum(partial_sum.astype(jnp.bfloat16), 'mp').astype(jnp.float32)  891 us
    all_gather x6, waiting for transfers between devices, layer_pass(): lax.all_gather(inputs, 'dp', axis=0, tiled=True)  140 us
    reduce_scatter x6, waiting for transfers between devices, layer_pass(): lax.psum_scatter(lax.dot_general(active, second_weight, (((1,), (second_d...  134 us
    dot_general x6, matrix products, layer_pass(): lax.dot_general(active, second_weight, (((1,), (second_dim,)), ((), ())),...  117 us
    dot_general x6, matrix products, layer_pass(): lax.dot_general(lax.all_gather(inputs, 'dp', axis=0, tiled=True), first_w...  101 us
    reduce_scatter x2, waiting for transfers between devices, lookup(): lax.psum_scatter(jnp.where(inside[:, None], fetched.astype(jnp.float32),...  59.4 us
  transfers between devices with their start and end apart: 23, of which 22 were waited for; matrix products, arithmetic and copies ran while one was open for 5% of the time, Pallas kernels for 0%

commit v1 on v0

--- a/solution.py
+++ b/solution.py
@@ -53,7 +53,9 @@
         (((1,), (first_dim,)), ((), ())),
         preferred_element_type=jnp.float32,
     )
-    summed = lax.psum(partial_sum.astype(jnp.bfloat16), "mp").astype(jnp.float32)
+    summed = jnp.sum(lax.all_gather(partial_sum.astype(jnp.bfloat16), "mp"), axis=0).astype(
+        jnp.float32
+    )
     active, kept = activate(summed)
     mixed = lax.psum_scatter(
         lax.dot_general(

time: 1520 us -> 2360 us (1.55)
  waiting for transfers between devices: 1230 us -> 1990 us
  other arithmetic: 19.2 us -> 90.7 us
    all_gather x0 -> x6, waiting for transfers between devices: none -> 1670 us  [layer_pass(): lax.all_gather(partial_sum.astype(jnp.bfloat16), 'mp')]
    psum x5 -> x0, waiting for transfers between devices: 891 us -> none  [layer_pass(): lax.psum(partial_sum.astype(jnp.bfloat16), 'mp').astype(jnp.float32)]
    reduce_sum x0 -> x6, other arithmetic: none -> 71.5 us  [layer_pass(): jnp.sum(lax.all_gather(partial_sum.astype(jnp.bfloat16), 'mp'), axis=0)]
  transfers between devices with their start and end apart: 23 -> 24, of which waited for: 22 -> 22; matrix products, arithmetic and copies ran while one was open for 5% -> 5% of each run, Pallas kernels for 0% -> 0%
where the time goes in v1:
time: 2360 us; the launch traced here: 2350 us
  waiting for transfers between devices  1990 us (84%)
  matrix products  222 us (9%)
  other arithmetic  90.7 us (4%)
    all_gather x6, waiting for transfers between devices, layer_pass(): lax.all_gather(partial_sum.astype(jnp.bfloat16), 'mp')  1670 us
    all_gather x6, waiting for transfers between devices, layer_pass(): lax.all_gather(inputs, 'dp', axis=0, tiled=True)  139 us
    dot_general x6, matrix products, layer_pass(): lax.dot_general(active, second_weight, (((1,), (second_dim,)), ((), ())),...  119 us
    reduce_scatter x6, waiting for transfers between devices, layer_pass(): lax.psum_scatter(lax.dot_general(active, second_weight, (((1,), (second_d...  118 us
    dot_general x6, matrix products, layer_pass(): lax.dot_general(lax.all_gather(inputs, 'dp', axis=0, tiled=True), first_w...  103 us
    reduce_sum x6, other arithmetic, layer_pass(): jnp.sum(lax.all_gather(partial_sum.astype(jnp.bfloat16), 'mp'), axis=0)  71.5 us
    reduce_scatter x2, waiting for transfers between devices, lookup(): lax.psum_scatter(jnp.where(inside[:, None], fetched.astype(jnp.float32),...  59.4 us
  transfers between devices with their start and end apart: 24, of which 22 were waited for; matrix products, arithmetic and copies ran while one was open for 5% of the time, Pallas kernels for 0%

profile of v1, /device:TPU:0, one launch (start us, length us, event | category | flops | bytes accessed | tf_op | source)
XLA Modules:
  0.0 2348.9 jit_solution(14837390863416743052)
XLA Ops:
  7.2 0.8 and_reduce_fusion.1
  8.0 0.8 broadcast_clamp_fusion
  8.8 10.1 gather_fusion
  19.0 1.3 select_convert_fusion.1
  20.3 31.3 %reduce-scatter.9.cloned.1.call-done = bf16[64,2048]{1,0:T(8,128)(2,1)} async-done(((bf16[256,2048]{1,0:T(8,128)(2,1)}), bf16[64,2048]{1,0:T(8,128)(2,1)}) %reduce-scatter.9.cloned.1.call-update) | async-done | bytes 262160 | tf_op jit(solution)/shard_map/reduce_scatter | solution.py:41
  51.7 1.7 broadcast_select_fusion.3
  53.4 27.2 %all-gather.20.cloned.1.call-done = bf16[256,2048]{1,0:T(8,128)(2,1)} async-done(((bf16[64,2048]{1,0:T(8,128)(2,1)}), bf16[256,2048]{1,0:T(8,128)(2,1)}) %all-gather.20.cloned.1.call-update) | async-done | bytes 1048592 | tf_op jit(solution)/shard_map/all_gather | solution.py:51
  80.6 16.7 fusion.24
  97.6 286.6 %all-gather.30.cloned.1.call-done = bf16[1024,8192]{1,0:T(8,128)(2,1)} async-done(((bf16[256,8192]{1,0:T(8,128)(2,1)}), bf16[1024,8192]{1,0:T(8,128)(2,1)}) %all-gather.30.cloned.1.call-update) | async-done | bytes 16777232 | tf_op jit(solution)/shard_map/all_gather | solution.py:56
  384.2 11.8 reduce_sum.72
  396.0 18.7 fusion.123
  414.8 10.3 gather_fusion.1
  425.1 1.3 select_convert_fusion
  426.5 14.5 reduce-scatter.11.cloned.1.call-done
  441.0 1.0 add_convert_fusion.4
  442.1 1.6 collective-permute-start
  443.7 28.1 %reduce-scatter.13.cloned.1.call-done = bf16[64,2048]{1,0:T(8,128)(2,1)} async-done(((bf16[256,2048]{1,0:T(8,128)(2,1)}), bf16[64,2048]{1,0:T(8,128)(2,1)}) %reduce-scatter.13.cloned.1.call-update) | async-done | bytes 262160 | tf_op jit(solution)/shard_map/reduce_scatter | solution.py:41
  471.7 1.7 broadcast_select_fusion.2
  473.7 26.8 %all-gather.22.cloned.1.call-done = bf16[256,2048]{1,0:T(8,128)(2,1)} async-done(((bf16[64,2048]{1,0:T(8,128)(2,1)}), bf16[256,2048]{1,0:T(8,128)(2,1)}) %all-gather.22.cloned.1.call-update) | async-done | bytes 1048592 | tf_op jit(solution)/shard_map/all_gather | solution.py:51
  500.5 16.6 fusion.27
  517.3 286.9 %all-gather.32.cloned.1.call-done = bf16[1024,8192]{1,0:T(8,128)(2,1)} async-done(((bf16[256,8192]{1,0:T(8,128)(2,1)}), bf16[1024,8192]{1,0:T(8,128)(2,1)}) %all-gather.32.cloned.1.call-update) | async-done | bytes 16777232 | tf_op jit(solution)/shard_map/all_gather | solution.py:56
  804.1 11.8 reduce_sum.73
  816.0 18.8 fusion.128
  834.9 0.7 slice_select_fusion
  835.7 25.4 %reduce-scatter.15.cloned.1.call-done = bf16[64,2048]{1,0:T(8,128)(2,1)} async-done(((bf16[256,2048]{1,0:T(8,128)(2,1)}), bf16[64,2048]{1,0:T(8,128)(2,1)}) %reduce-scatter.15.cloned.1.call-update) | async-done | bytes 262160 | tf_op jit(solution)/shard_map/reduce_scatter | solution.py:60
  861.1 1.8 select_bitcast_fusion.1
  863.6 1.6 collective-permute-start.1
  865.1 1.1 collective-permute-done.1
  867.0 0.7 broadcast_select_fusion.1
  868.2 21.2 all-gather.36.cloned.1.call-done
  889.5 17.2 fusion.33
  906.7 11.0 all-gather.24.cloned.1.call-done
  917.7 19.0 fusion.30
  936.9 269.2 %all-gather.38.cloned.1.call-done = bf16[1024,8192]{1,0:T(8,128)(2,1)} async-done(((bf16[256,8192]{1,0:T(8,128)(2,1)}), bf16[1024,8192]{1,0:T(8,128)(2,1)}) %all-gather.38.cloned.1.call-update) | async-done | bytes 16777232 | tf_op jit(solution)/shard_map/all_gather | solution.py:56
  1206.0 12.5 reduce_sum.75
  1218.5 273.9 %all-gather.34.cloned.1.call-done = bf16[1024,8192]{1,0:T(8,128)(2,1)} async-done(((bf16[256,8192]{1,0:T(8,128)(2,1)}), bf16[1024,8192]{1,0:T(8,128)(2,1)}) %all-gather.34.cloned.1.call-update) | async-done | bytes 16777232 | tf_op jit(solution)/shard_map/all_gather | solution.py:56
  1492.4 11.8 reduce_sum.74
  1504.3 19.9 fusion.108
  1524.3 26.2 %reduce-scatter.19.cloned.1.call-done = bf16[64,2048]{1,0:T(8,128)(2,1)} async-done(((bf16[256,2048]{1,0:T(8,128)(2,1)}), bf16[64,2048]{1,0:T(8,128)(2,1)}) %reduce-scatter.19.cloned.1.call-update) | async-done | bytes 262160 | tf_op jit(solution)/shard_map/reduce_scatter | solution.py:60
  1550.5 1.0 fusion.139
  1551.5 1.3 collective-permute-start.2
  1552.8 2.1 collective-permute-done.2
  1554.9 0.7 bitcast_select_fusion
  1555.7 26.6 %all-gather.26.cloned.1.call-done = bf16[256,2048]{1,0:T(8,128)(2,1)} async-done(((bf16[64,2048]{1,0:T(8,128)(2,1)}), bf16[256,2048]{1,0:T(8,128)(2,1)}) %all-gather.26.cloned.1.call-update) | async-done | bytes 1048592 | tf_op jit(solution)/shard_map/all_gather | solution.py:51
  1582.4 16.9 fusion.36
  1599.5 286.7 %all-gather.40.cloned.1.call-done = bf16[1024,8192]{1,0:T(8,128)(2,1)} async-done(((bf16[256,8192]{1,0:T(8,128)(2,1)}), bf16[1024,8192]{1,0:T(8,128)(2,1)}) %all-gather.40.cloned.1.call-update) | async-done | bytes 16777232 | tf_op jit(solution)/shard_map/all_gather | solution.py:56
  1886.2 11.7 reduce_sum.76
  1897.9 20.0 fusion.113
  1918.0 26.2 %reduce-scatter.21.cloned.1.call-done = bf16[64,2048]{1,0:T(8,128)(2,1)} async-done(((bf16[256,2048]{1,0:T(8,128)(2,1)}), bf16[64,2048]{1,0:T(8,128)(2,1)}) %reduce-scatter.21.cloned.1.call-update) | async-done | bytes 262160 | tf_op jit(solution)/shard_map/reduce_scatter | solution.py:60
  1944.2 1.1 select_bitcast_fusion
  1945.3 1.3 collective-permute-start.3
  1946.6 2.1 collective-permute-done.3
  1948.7 0.7 broadcast_select_fusion
  1949.5 26.6 %all-gather.28.cloned.1.call-done = bf16[256,2048]{1,0:T(8,128)(2,1)} async-done(((bf16[64,2048]{1,0:T(8,128)(2,1)}), bf16[256,2048]{1,0:T(8,128)(2,1)}) %all-gather.28.cloned.1.call-update) | async-done | bytes 1048592 | tf_op jit(solution)/shard_map/all_gather | solution.py:51
  1976.1 16.9 fusion.39
  1993.3 21.1 fusion.133
  2014.5 265.5 %all-gather.42.cloned.1.call-done = bf16[1024,8192]{1,0:T(8,128)(2,1)} async-done(((bf16[256,8192]{1,0:T(8,128)(2,1)}), bf16[1024,8192]{1,0:T(8,128)(2,1)}) %all-gather.42.cloned.1.call-update) | async-done | bytes 16777232 | tf_op jit(solution)/shard_map/all_gather | solution.py:56
  2279.9 11.9 reduce_sum.77
  2291.8 20.4 fusion.118
  2312.3 1.1 fusion.141
  2313.4 0.8 maximum_bitcast_fusion
  2314.2 25.4 %reduce-scatter.23.cloned.1.call-done = bf16[64,2048]{1,0:T(8,128)(2,1)} async-done(((bf16[256,2048]{1,0:T(8,128)(2,1)}), bf16[64,2048]{1,0:T(8,128)(2,1)}) %reduce-scatter.23.cloned.1.call-update) | async-done | bytes 262160 | tf_op jit(solution)/shard_map/reduce_scatter | solution.py:60
  2339.7 1.1 fusion.143
  2340.8 0.8 maximum_bitcast_fusion.1
  (66 shorter events, 4.2 us)
Async XLA Ops:
  7.2 44.5 %reduce-scatter.9.cloned.1.call-start = ((), (), s32[]{:S(2)}) async-start(), calls=%async_computation.8 | async-start | bytes 1310720 | tf_op jit(solution)/shard_map/reduce_scatter | solution.py:41
  20.3 60.3 %all-gather.20.cloned.1.call-start = ((), (), s32[]{:S(2)}) async-start(), calls=%async_computation.9 | async-start | bytes 1310720 | tf_op jit(solution)/shard_map/all_gather | solution.py:51
  53.4 330.9 %all-gather.30.cloned.1.call-start = ((), (), s32[]{:S(2)}) async-start(), calls=%async_computation.21 | async-start | bytes 20971520 | tf_op jit(solution)/shard_map/all_gather | solution.py:56
  97.3 343.7 %reduce-scatter.11.cloned.1.call-start = ((), (), s32[]{:S(2)}) async-start(), calls=%async_computation.10 | async-start | bytes 1310720 | tf_op jit(solution)/shard_map/reduce_scatter | solution.py:60
  414.7 26.3 %copy-start.8 = (bf16[64,2048]{1,0:T(8,128)(2,1)S(1)}, bf16[64,2048]{1,0:T(8,128)(2,1)}, u32[]{:S(2)}) copy-start(bf16[64,2048]{1,0:T(8,128)(2,1)} %reduce-scatter.9.cloned.1.call-done) | copy-start | bytes 786436
  414.7 57.0 %reduce-scatter.13.cloned.1.call-start = ((), (), s32[]{:S(2)}) async-start(), calls=%async_computation.11 | async-start | bytes 1310720 | tf_op jit(solution)/shard_map/reduce_scatter | solution.py:41
  426.5 74.1 %all-gather.22.cloned.1.call-start = ((), (), s32[]{:S(2)}) async-start(), calls=%async_computation.12 | async-start | bytes 1310720 | tf_op jit(solution)/shard_map/all_gather | solution.py:51
  442.1 29.7 %collective-permute-start = (bf16[64,2048]{1,0:T(8,128)(2,1)S(1)}, bf16[64,2048]{1,0:T(8,128)(2,1)S(1)}, u32[]{:S(2)}, u32[]{:S(2)}) collective-permute-start(bf16[64,2048]{1,0:T(8,128)(2,1)S(1)} %add_convert_fusion.4), channel_id=1, source_target_pairs={{0,16},{1,17},{2,18},{3,19},{4,20},{5,21},{6,22},{7,23},{8,24},{9,... | collective-permute-start | bytes 786440 | tf_op jit(solution)/shard_map/ppermute | solution.py:13
  473.4 330.7 %all-gather.32.cloned.1.call-start = ((), (), s32[]{:S(2)}) async-start(), calls=%async_computation.22 | async-start | bytes 20971520 | tf_op jit(solution)/shard_map/all_gather | solution.py:56
  517.2 343.9 %reduce-scatter.15.cloned.1.call-start = ((), (), s32[]{:S(2)}) async-start(), calls=%async_computation.13 | async-start | bytes 1310720 | tf_op jit(solution)/shard_map/reduce_scatter | solution.py:60
  815.9 18.9 copy-start.2
  815.9 45.1 %copy-start = (bf16[64,2048]{1,0:T(8,128)(2,1)S(1)}, bf16[64,2048]{1,0:T(8,128)(2,1)}, u32[]{:S(2)}) copy-start(bf16[64,2048]{1,0:T(8,128)(2,1)} %broadcast_select_fusion.2) | copy-start | bytes 786436
  834.8 54.7 %all-gather.36.cloned.1.call-start = ((), (), s32[]{:S(2)}) async-start(), calls=%async_computation.24 | async-start | bytes 1310720 | tf_op jit(solution)/shard_map/all_gather | solution.py:51
  835.6 82.1 %all-gather.24.cloned.1.call-start = ((), (), s32[]{:S(2)}) async-start(), calls=%async_computation.14 | async-start | bytes 1310720 | tf_op jit(solution)/shard_map/all_gather | solution.py:51
  862.9 0.7 copy-start.4
  863.6 2.7 collective-permute-start.1
  866.3 0.7 copy-start.6
  867.7 338.3 %all-gather.38.cloned.1.call-start = ((), (), s32[]{:S(2)}) async-start(), calls=%async_computation.25 | async-start | bytes 20971520 | tf_op jit(solution)/shard_map/all_gather | solution.py:56
  906.6 585.8 %all-gather.34.cloned.1.call-start = ((), (), s32[]{:S(2)}) async-start(), calls=%async_computation.23 | async-start | bytes 20971520 | tf_op jit(solution)/shard_map/all_gather | solution.py:56
  936.7 613.8 %reduce-scatter.19.cloned.1.call-start = ((), (), s32[]{:S(2)}) async-start(), calls=%async_computation.16 | async-start | bytes 1310720 | tf_op jit(solution)/shard_map/reduce_scatter | solution.py:60
  1524.2 58.2 %all-gather.26.cloned.1.call-start = ((), (), s32[]{:S(2)}) async-start(), calls=%async_computation.17 | async-start | bytes 1310720 | tf_op jit(solution)/shard_map/all_gather | solution.py:51
  1551.5 3.4 collective-permute-start.2
  1555.7 330.5 %all-gather.40.cloned.1.call-start = ((), (), s32[]{:S(2)}) async-start(), calls=%async_computation.26 | async-start | bytes 20971520 | tf_op jit(solution)/shard_map/all_gather | solution.py:56
  1599.2 344.9 %reduce-scatter.21.cloned.1.call-start = ((), (), s32[]{:S(2)}) async-start(), calls=%async_computation.18 | async-start | bytes 1310720 | tf_op jit(solution)/shard_map/reduce_scatter | solution.py:60
  1897.9 46.3 %copy-start.1 = (bf16[64,2048]{1,0:T(8,128)(2,1)S(1)}, bf16[64,2048]{1,0:T(8,128)(2,1)}, u32[]{:S(2)}) copy-start(bf16[64,2048]{1,0:T(8,128)(2,1)} %bitcast_select_fusion) | copy-start | bytes 786436
  1917.9 58.2 %all-gather.28.cloned.1.call-start = ((), (), s32[]{:S(2)}) async-start(), calls=%async_computation.19 | async-start | bytes 1310720 | tf_op jit(solution)/shard_map/all_gather | solution.py:51
  1945.3 3.4 collective-permute-start.3
  1949.5 330.5 %all-gather.42.cloned.1.call-start = ((), (), s32[]{:S(2)}) async-start(), calls=%async_computation.27 | async-start | bytes 20971520 | tf_op jit(solution)/shard_map/all_gather | solution.py:56
  1993.0 319.3 %reduce-scatter.17.cloned.1.call-start = ((), (), s32[]{:S(2)}) async-start(), calls=%async_computation.15 | async-start | bytes 1310720 | tf_op jit(solution)/shard_map/reduce_scatter | solution.py:60
  2014.4 325.3 %reduce-scatter.23.cloned.1.call-start = ((), (), s32[]{:S(2)}) async-start(), calls=%async_computation.20 | async-start | bytes 1310720 | tf_op jit(solution)/shard_map/reduce_scatter | solution.py:60
  2291.8 20.5 copy-start.5
  2291.8 20.5 copy-start.7
  2291.8 21.6 copy-start.3
Sparse Core Ops, SparseCore 0:
  20.4 31.2 reduce-scatter.8
  54.1 26.4 all-gather.19
  97.4 286.7 all-gather.29
  414.9 26.0 reduce-scatter.10
  443.8 27.9 reduce-scatter.12
  474.0 26.4 all-gather.21
  517.3 286.7 all-gather.31
  834.9 26.1 reduce-scatter.14
  862.9 26.4 all-gather.35
  891.2 26.4 all-gather.23
  919.3 286.7 all-gather.37
  1207.5 284.9 all-gather.33
  1524.3 26.0 reduce-scatter.18
  1555.8 26.5 all-gather.25
  1599.4 286.7 all-gather.39
  1918.0 26.1 reduce-scatter.20
  1949.6 26.4 all-gather.27
  1993.1 286.7 all-gather.41
  2282.8 26.0 reduce-scatter.16
  2312.4 27.2 reduce-scatter.22
